TPU v7x, 32 devices: a whole 2x2x4 slice. The times are simulated.
32 devices in a mesh: tok: 16 (over z, y, core), tp: 2 (over x).
Axes of the slice: x: 2, y: 2, z: 4, core: 2. Of those that a mesh axis runs over, the one named last changes fastest.
Arguments:
- hidden_in: bfloat16 [4096, 4096], P('tok', 'tp'), may hold values from -6 to 6
- norm_gain: float32 [4096], replicated, may hold values from 0.5 to 9, as said below
- w_query: bfloat16 [4096, 4096], P(None, 'tp'), may hold values from -0.09375 to 0.09375
- w_key: bfloat16 [4096, 1024], P(None, 'tp'), may hold values from -0.09375 to 0.09375
- w_value: bfloat16 [4096, 1024], P(None, 'tp'), may hold values from -0.09375 to 0.09375
- w_out: bfloat16 [4096, 4096], P('tp'), may hold values from -0.5 to 0.5
- doc_ids: int32 [4096], replicated, may hold values from 0 to 3, never falling along the last dimension, each value on 1 to 3072 neighbouring positions
Outputs:
- hidden_out: bfloat16 [4096, 4096], P('tok', 'tp')
- joint_cov: float32 [2, 4096, 2, 4096], P(None, 'tok', None, 'tp')
Inputs may be any that keep to these rules, and one draw needn't show every extreme that they name: `norm_gain`: each channel's gain is positive. `doc_ids`: document numbers never fall along the tokens; a document holds 1 to 3072 tokens.
All inputs are finite; a program needn't handle non-finite values.
Results may differ from a plain program's by a relative error of at most 0.013.
The roundings to bfloat16 on the way count: a program that leaves them out, or rounds other values in their place, can miss the bound.
Values may be sent and summed in bfloat16 or wider, within the bound.
A program may use at most 192 MiB of HBM per device.

v0:
```python
import jax
import jax.numpy as jnp
from jax import lax
from jax.sharding import PartitionSpec as P

HS = 128


epsilon = 1e-05
rope_base = 500000.0


def broadcast(block, axis, source):
    block = jnp.where(lax.axis_index(axis) == source, block, jnp.zeros_like(block))
    return lax.psum(block, axis)


def rotate(vectors, positions):
    half_dim = vectors.shape[-1] // 2
    inv_freq = rope_base ** (-(jnp.arange(half_dim, dtype=jnp.float32) * 2.0) / vectors.shape[-1])
    angles = positions.astype(jnp.float32)[:, None] * inv_freq[None, :]
    cosine = jnp.cos(angles)[:, None, :]
    sine_part = jnp.sin(angles)[:, None, :]
    first_half = vectors[..., :half_dim]
    second_half = vectors[..., half_dim:]
    return jnp.concatenate(
        [
            first_half * cosine - second_half * sine_part,
            second_half * cosine + first_half * sine_part,
        ],
        axis=-1,
    )


def on_device(hidden_in, norm_gain, w_query, w_key, w_value, w_out, doc_ids):
    tok_rows = hidden_in.shape[0]
    col_width = hidden_in.shape[1]
    tok_count = lax.axis_size("tok")
    tok_index = lax.axis_index("tok")
    all_rows = tok_rows * tok_count
    full_in = lax.all_gather(hidden_in, "tp", axis=1, tiled=True)
    model_width = full_in.shape[1]
    row_width = model_width // tok_count
    widened = full_in.astype(jnp.float32)
    factor = lax.rsqrt(jnp.mean(widened * widened, axis=1, keepdims=True) + epsilon)
    normed = (widened * factor * norm_gain[None, :]).astype(jnp.bfloat16)
    kv_heads = w_key.shape[1] // HS
    groups = w_query.shape[1] // w_key.shape[1]
    first_row = tok_index * tok_rows
    positions = first_row + jnp.arange(tok_rows, dtype=jnp.int32)
    key_local = rotate(
        jnp.dot(normed, w_key, preferred_element_type=jnp.float32).reshape(tok_rows, kv_heads, HS),
        positions % all_rows,
    )
    key_local = key_local.astype(jnp.bfloat16).reshape(tok_rows, kv_heads * HS)
    value_local = jnp.dot(normed, w_value, preferred_element_type=jnp.float32).astype(jnp.bfloat16)
    key_rows, value_rows = (
        lax.all_gather(key_local, "tok", axis=0, tiled=True),
        lax.all_gather(value_local, "tok", axis=0, tiled=True),
    )
    queries = rotate(
        jnp.dot(normed, w_query, preferred_element_type=jnp.float32).reshape(
            tok_rows, kv_heads * groups, HS
        ),
        positions % all_rows,
    )
    queries = queries.astype(jnp.bfloat16).reshape(tok_rows, kv_heads, groups, HS)
    key_seq = key_rows.reshape(all_rows, kv_heads, HS)
    value_seq = value_rows.reshape(all_rows, kv_heads, HS)
    key_pos = jnp.arange(all_rows, dtype=jnp.int32)
    query_doc = lax.dynamic_slice_in_dim(doc_ids, first_row, tok_rows, 0)
    allowed = (query_doc[:, None] == doc_ids[None, :]) & (key_pos[None, :] <= positions[:, None])
    scores = jnp.einsum(
        "qhgd,khd->hgqk", queries, key_seq, preferred_element_type=jnp.float32
    ) * HS ** (-0.5)
    scores = jnp.where(allowed[None, None], scores, -jnp.inf)
    row_max = jnp.max(scores, axis=-1, keepdims=True)
    weights = jnp.exp(scores - row_max)
    weight_sum = jnp.sum(weights, axis=-1, keepdims=True)
    blended = (
        jnp.einsum(
            "hgqk,khd->hgqd",
            weights.astype(jnp.bfloat16),
            value_seq,
            preferred_element_type=jnp.float32,
        )
        / weight_sum
    )
    attended = (
        jnp.transpose(blended, (2, 0, 1, 3))
        .astype(jnp.bfloat16)
        .reshape(tok_rows, kv_heads * groups * HS)
    )
    partial_out = jnp.dot(attended, w_out, preferred_element_type=jnp.float32)
    summed = lax.psum_scatter(partial_out, "tp", scatter_dimension=1, tiled=True)
    hidden_out = (hidden_in.astype(jnp.float32) + summed).astype(jnp.bfloat16)
    columns = lax.all_gather(jnp.stack([hidden_in, hidden_out], axis=1), "tok", axis=0, tiled=True)
    offset = tok_index * row_width % col_width
    owner_rank = tok_index * row_width // col_width
    own_rows = lax.dynamic_slice_in_dim(columns, offset, row_width, 2)
    row_block = broadcast(own_rows, "tp", owner_rank).reshape(all_rows, 2 * row_width)
    flat_cols = columns.reshape(all_rows, 2 * col_width)
    gram_block = lax.dot_general(
        row_block, flat_cols, (((0,), (0,)), ((), ())), preferred_element_type=jnp.float32
    )
    col_sum = jnp.sum(flat_cols, axis=0, dtype=jnp.float32)
    row_mean = jnp.sum(row_block, axis=0, dtype=jnp.float32) / all_rows
    col_mean = col_sum / all_rows
    joint_cov = (gram_block / all_rows - row_mean[:, None] * col_mean[None, :]).reshape(
        2, row_width, 2, col_width
    )
    return (hidden_out, joint_cov)


def solution(mesh):
    return jax.shard_map(
        on_device,
        mesh=mesh,
        in_specs=(
            P("tok", "tp"),
            P(),
            P(None, "tp"),
            P(None, "tp"),
            P(None, "tp"),
            P("tp", None),
            P(),
        ),
        out_specs=(P("tok", "tp"), P(None, "tok", None, "tp")),
        check_vma=False,
    )
```

profile of v0, /device:TPU:0, one launch (start us, length us, event | category | flops | bytes accessed | tf_op | source)
XLA Modules:
  0.0 588.9 jit_solution(13531846354874264925)
XLA Ops:
  7.2 0.0 all-gather.5.cloned.1.call-start
  7.2 0.7 all-gather.5.cloned.1.call-update
  7.9 0.0 all-gather.7.cloned.1.call-start
  8.0 0.5 multiply_cosine_fusion
  8.5 36.8 %all-gather.5.cloned.1.call-done = bf16[256,4096]{1,0:T(8,128)(2,1)} async-done(((bf16[256,2048]{1,0:T(8,128)(2,1)}), bf16[256,4096]{1,0:T(8,128)(2,1)}) %all-gather.5.cloned.1.call-update) | async-done | bytes 2097168 | tf_op jit(solution)/shard_map/all_gather | solution.py:41
  45.4 2.1 fusion.6
  47.5 4.1 fusion.24
  51.6 0.2 reshape.184
  51.8 0.5 subtract_convert_fusion.1
  52.3 0.4 pad_maximum_fusion.1
  52.7 0.9 copy.13
  53.5 0.0 all-gather.7.cloned.1.call-update
  53.6 0.0 all-gather.9.cloned.1.call-start
  53.6 0.1 dynamic_slice.6
  53.7 1.9 fusion.9
  55.6 8.3 %convolution_bitcast_fusion = f32[32,8,16,128]{3,1,2,0:T(8,128)S(1)} fusion(bf16[4096,2048]{1,0:T(8,128)(2,1)} %param.9, bf16[256,4096]{1,0:T(8,128)(2,1)S(1)} %copy-done.2, f32[4096]{0:T(1024)S(1)} %copy-done.5, f32[256]{0:T(256)S(1)} %add_rsqrt_fusion), kind=kOutput, calls=%fused_computation.24 | convolution fusion | flops 4299161600 | bytes 20988928 | tf_op jit(solution)/shard_map/dot_general | solution.py:62
  63.9 0.4 copy.27
  64.3 0.0 copy-start.4
  64.3 0.8 subtract_convert_fusion
  65.1 1.2 copy.14
  66.3 1.2 copy.15
  67.5 2.0 convolution_convert_fusion
  69.5 0.0 all-gather.9.cloned.1.call-update
  69.6 0.2 reduce-scatter.2.cloned.1.call-start
  69.8 36.4 %all-gather.7.cloned.1.call-done = bf16[4096,512]{0,1:T(8,128)(2,1)} async-done(((bf16[256,512]{0,1:T(8,128)(2,1)}), bf16[4096,512]{0,1:T(8,128)(2,1)}) %all-gather.7.cloned.1.call-update) | async-done | bytes 4194320 | tf_op jit(solution)/shard_map/all_gather | solution.py:58
  106.2 28.9 %fusion.2 = (f32[4,4,256]{2,1,0:T(4,128)S(1)}, f32[4,4096,256,4]{2,1,3,0:T(8,128)}) fusion(pred[256,4096]{0,1:T(8,128)(4,1)S(1)} %fusion.9, bf16[4096,4,128,1]{0,2,3,1:T(8,128)(2,1)} %bitcast.65, bf16[256,4,4,64]{3,0,2,1:T(8,128)(2,1)} %bitcast.60, bf16[256,4,4,64]{3,0,2,1:T(8,128)(2,1)} %bitcast.59), kind=kOutput, calls=%fused_computation.5 | convolution fusion | flops 4347392000 | bytes 73416704 | tf_op jit(solution)/shard_map/qhgd,khd->hgqk/dot_general | solution.py:73
  135.2 22.1 %fusion = f32[4,4,256]{2,1,0:T(4,128)S(1)} fusion(f32[4,4096,256,4]{2,1,3,0:T(8,128)} %get-tuple-element.9, f32[4,4,256]{2,1,0:T(4,128)S(1)} %get-tuple-element.8, pred[256,4096]{0,1:T(8,128)(4,1)S(1)} %fusion.9), kind=kLoop, calls=%fused_computation.3 | loop fusion | flops 67104768 | bytes 68190208 | tf_op jit(solution)/shard_map/reduce_sum | solution.py:79
  157.3 0.0 all-gather.9.cloned.1.call-done
  157.3 6.3 %copy.26 = bf16[4096,512]{0,1:T(8,128)(2,1)} copy(bf16[4096,512]{1,0:T(8,128)(2,1)} %all-gather.9.cloned.1.call-done) | data formatting | bytes 8388608 | tf_op jit(solution)/shard_map/reshape | solution.py:69
  163.6 25.5 %fusion.10 = bf16[256,4,4,128]{0,3,2,1:T(8,128)(2,1)S(1)} fusion(bf16[4096,4,128,1]{0,2,3,1:T(8,128)(2,1)} %bitcast.55, f32[4,4096,256,4]{2,1,3,0:T(8,128)} %get-tuple-element.9, f32[4,4,256]{2,1,0:T(4,128)S(1)} %get-tuple-element.8, pred[256,4096]{0,1:T(8,128)(4,1)S(1)} %fusion.9, f32[256,4,4]{0,2,1:T(4,128)S(1)} %bitcast.63), kind=kOutput, calls=%fused_computation.20 | convolution fusion | flops 4363124736 | bytes 73433088 | tf_op jit(solution)/shard_map/hgqk,khd->hgqd/dot_general | solution.py:81
  189.2 10.4 %fusion.26 = f32[256,4096]{1,0:T(8,128)} fusion(bf16[256,2048]{0,1:T(8,128)(2,1)S(1)} %bitcast.58, bf16[2048,4096]{1,0:T(8,128)(2,1)} %param.12), kind=kOutput, calls=%fused_computation.49 | convolution fusion | flops 4294967296 | bytes 22020096 | tf_op jit(solution)/shard_map/dot_general | solution.py:94
  199.6 0.0 reduce-scatter.2.cloned.1.call-update
  199.6 0.0 all-gather.11.cloned.1.call-start
  199.7 52.7 %reduce-scatter.2.cloned.1.call-done = f32[256,2048]{1,0:T(8,128)} async-done(((f32[256,4096]{1,0:T(8,128)}), f32[256,2048]{1,0:T(8,128)}) %reduce-scatter.2.cloned.1.call-update) | async-done | bytes 2097168 | tf_op jit(solution)/shard_map/reduce_scatter | solution.py:95
  252.4 1.9 add_convert_fusion
  254.3 1.7 pad_maximum_fusion
  256.0 0.0 all-gather.11.cloned.1.call-update
  256.0 0.0 all-reduce.2.cloned.1.call-start
  256.1 168.1 %all-gather.11.cloned.1.call-done = bf16[4096,2,2048]{2,0,1:T(8,128)(2,1)} async-done(((bf16[256,2,2048]{2,0,1:T(8,128)(2,1)}), bf16[4096,2,2048]{2,0,1:T(8,128)(2,1)}) %all-gather.11.cloned.1.call-update) | async-done | bytes 33554448 | tf_op jit(solution)/shard_map/all_gather | solution.py:97
  424.2 4.9 dynamic-slice_select_fusion
  429.1 0.0 all-reduce.2.cloned.1.call-update
  429.2 12.4 %convert_reduce_fusion = f32[2,2048]{1,0:T(2,128)S(1)} fusion(bf16[4096,2,2048]{2,0,1:T(8,128)(2,1)} %all-gather.11.cloned.1.call-done), kind=kLoop, calls=%fused_computation.1 | loop fusion | flops 33550336 | bytes 33570816 | tf_op jit(solution)/shard_map/reduce_sum | solution.py:106
  441.6 40.5 %copy.20 = bf16[4096,2,2048]{0,2,1:T(8,128)(2,1)} copy(bf16[4096,2,2048]{2,0,1:T(8,128)(2,1)} %all-gather.11.cloned.1.call-done) | data formatting | bytes 67108864 | tf_op jit(solution)/shard_map/all_gather | solution.py:97
  482.0 55.2 %all-reduce.2.cloned.1.call-done = bf16[4096,2,256]{2,0,1:T(8,128)(2,1)} async-done(((bf16[4096,2,256]{2,0,1:T(8,128)(2,1)}), bf16[4096,2,256]{2,0,1:T(8,128)(2,1)}) %all-reduce.2.cloned.1.call-update) | async-done | bytes 4194320 | tf_op jit(solution)/shard_map/psum | solution.py:15
  537.2 2.8 convert_reduce_fusion.1
  540.0 6.3 %copy.19 = bf16[4096,2,256]{0,2,1:T(8,128)(2,1)} copy(bf16[4096,2,256]{2,0,1:T(8,128)(2,1)} %all-reduce.2.cloned.1.call-done) | data formatting | bytes 8388608 | tf_op jit(solution)/shard_map/psum | solution.py:15
  546.3 24.0 %multiply_subtract_fusion = f32[512,4096]{1,0:T(8,128)} fusion(bf16[4096,512]{0,1:T(8,128)(2,1)} %bitcast.56, bf16[4096,4096]{0,1:T(8,128)(2,1)} %bitcast.52, f32[4096]{0:T(1024)S(1)} %bitcast.62, f32[512]{0:T(512)S(1)} %bitcast.64), kind=kOutput, calls=%fused_computation.8 | convolution fusion | flops 17186160640 | bytes 46155776 | tf_op jit(solution)/shard_map/dot_general | solution.py:103
  570.4 11.7 %reshape.191 = f32[2,256,2,2048]{3,2,1,0:T(2,128)} reshape(f32[512,4096]{1,0:T(8,128)} %multiply_subtract_fusion) | data formatting | bytes 16777216 | tf_op jit(solution)/shard_map/reshape | solution.py:109
  (19 shorter events, 0.1 us)
Async XLA Ops:
  7.2 38.2 %all-gather.5.cloned.1.call-start = ((), (), s32[]{:S(2)}) async-start(), calls=%async_computation.1 | async-start | bytes 3145728 | tf_op jit(solution)/shard_map/all_gather | solution.py:41
  7.9 98.3 %all-gather.7.cloned.1.call-start = ((), (), s32[]{:S(2)}) async-start(), calls=%async_computation.2 | async-start | bytes 4456448 | tf_op jit(solution)/shard_map/all_gather | solution.py:58
  51.6 2.0 copy-start.3
  51.6 4.0 copy-start.2
  51.6 4.0 copy-start.5
  53.6 103.7 %all-gather.9.cloned.1.call-start = ((), (), s32[]{:S(2)}) async-start(), calls=%async_computation.3 | async-start | bytes 4456448 | tf_op jit(solution)/shard_map/all_gather | solution.py:59
  64.3 3.3 copy-start.4
  69.6 182.8 %reduce-scatter.2.cloned.1.call-start = ((), (), s32[]{:S(2)}) async-start(), calls=%async_computation.4 | async-start | bytes 6291456 | tf_op jit(solution)/shard_map/reduce_scatter | solution.py:95
  199.6 52.8 %copy-start = (bf16[256,2048]{1,0:T(8,128)(2,1)S(1)}, bf16[256,2048]{1,0:T(8,128)(2,1)}, u32[]{:S(2)}) copy-start(bf16[256,2048]{1,0:T(8,128)(2,1)} %param.7) | copy-start | bytes 3145732
  199.6 224.6 %all-gather.11.cloned.1.call-start = ((), (), s32[]{:S(2)}) async-start(), calls=%async_computation.5 | async-start | bytes 35651584 | tf_op jit(solution)/shard_map/all_gather | solution.py:97
  254.3 174.8 %copy-start.1 = (bf16[256,2048]{1,0:T(8,128)(2,1)}, bf16[256,2048]{1,0:T(8,128)(2,1)S(1)}, u32[]{:S(2)}) copy-start(bf16[256,2048]{1,0:T(8,128)(2,1)S(1)} %add_convert_fusion) | copy-start | bytes 3145732
  256.0 281.2 %all-reduce.2.cloned.1.call-start = ((), (), s32[]{:S(2)}) async-start(), calls=%async_computation.6 | async-start | bytes 8388608 | tf_op jit(solution)/shard_map/psum | solution.py:15
Sparse Core Ops, SparseCore 0:
  9.5 35.8 all-gather.4
  53.7 52.4 all-gather.6
  108.4 48.5 all-gather.8
  199.7 52.6 reduce-scatter.1
  256.1 168.0 all-gather.10
  429.3 107.8 all-reduce.1
where the time goes:
time: 591 us; the launch traced here: 589 us
  waiting for transfers between devices  350 us (59%)
  matrix products  103 us (17%)
  local copies, waits for them, and re-layouts  68.9 us (12%)
  other arithmetic  51.8 us (9%)
  between operations  14.4 us (2%)
    all_gather x1, waiting for transfers between devices, on_device(): lax.all_gather(jnp.stack([hidden_in, hidden_out], axis=1), 'tok', axis=0,...  168 us
    psum x1, waiting for transfers between devices, broadcast(): return lax.psum(block, axis)  55.2 us
    reduce_scatter x1, waiting for transfers between devices, on_device(): lax.psum_scatter(partial_out, 'tp', scatter_dimension=1, tiled=True)  52.7 us
    all_gather x1, local copies, waits for them, and re-layouts, on_device(): lax.all_gather(jnp.stack([hidden_in, hidden_out], axis=1), 'tok', axis=0,...  40.5 us
    all_gather x1, waiting for transfers between devices, on_device(): full_in = lax.all_gather(hidden_in, 'tp', axis=1, tiled=True)  36.8 us
    all_gather x1, waiting for transfers between devices, on_device(): lax.all_gather(key_local, 'tok', axis=0, tiled=True)  36.4 us
    dot_general x1, matrix products, on_device(): jnp.einsum('qhgd,khd->hgqk', queries, key_seq, preferred_element_type=jnp...  28.9 us
    dot_general x1, matrix products, on_device(): jnp.einsum('hgqk,khd->hgqd', weights.astype(jnp.bfloat16), value_seq, pre...  25.5 us
  transfers between devices with their start and end apart: 6, of which 5 were waited for; matrix products, arithmetic and copies ran while one was open for 20% of the time, Pallas kernels for 0%

commit v1 on v0

v1 whole, which is shorter than its diff:
```python
import functools
import math

import jax
import jax.numpy as jnp
from jax import lax
from jax.experimental import pallas as pl
from jax.experimental.pallas import tpu as pltpu
from jax.sharding import PartitionSpec as P

HS = 128
epsilon = 1e-05
rope_base = 500000.0
VMEM_LIMIT = 60 * 1024 * 1024


def rotate(vectors, positions):
    half_dim = vectors.shape[-1] // 2
    inv_freq = rope_base ** (-(jnp.arange(half_dim, dtype=jnp.float32) * 2.0) / vectors.shape[-1])
    angles = positions.astype(jnp.float32)[:, None] * inv_freq[None, :]
    cosine = jnp.cos(angles)[:, None, :]
    sine_part = jnp.sin(angles)[:, None, :]
    first_half = vectors[..., :half_dim]
    second_half = vectors[..., half_dim:]
    return jnp.concatenate(
        [
            first_half * cosine - second_half * sine_part,
            second_half * cosine + first_half * sine_part,
        ],
        axis=-1,
    )


def attend_kernel(groups, block, bounds, q_ref, k_ref, v_ref, lo_ref, out_ref, s_ref, m_ref, l_ref, acc_ref):
    rows = q_ref.shape[0]
    first_row = bounds[0]
    scale = HS ** (-0.5) * math.log2(math.e)
    start = bounds[1] // block
    stop = (first_row + rows + block - 1) // block
    lanes = 128
    m_ref[...] = jnp.full_like(m_ref, -jnp.inf)
    l_ref[...] = jnp.zeros_like(l_ref)
    acc_ref[...] = jnp.zeros_like(acc_ref)

    @pl.loop(start, stop)
    def _(step):
        first_key = pl.multiple_of(step * block, block)
        keys = k_ref[pl.ds(first_key, block), :]
        key_pos = first_key + lax.broadcasted_iota(jnp.int32, (rows, block), 1)
        query_pos = first_row + lax.broadcasted_iota(jnp.int32, (rows, block), 0)
        allowed = (key_pos >= lo_ref[:, :1]) & (key_pos <= query_pos)
        for head in range(groups):
            part = pl.ds(head * rows, rows)
            s = lax.dot_general(
                q_ref[:, head * HS:(head + 1) * HS], keys,
                (((1,), (1,)), ((), ())), preferred_element_type=jnp.float32,
            ) * scale
            s = jnp.where(allowed, s, -jnp.inf)
            s_ref[step, part, :] = s
            top = m_ref[part, :]
            for piece in range(block // lanes):
                top = jnp.maximum(top, s[:, piece * lanes:(piece + 1) * lanes])
            m_ref[part, :] = top

    m_ref[...] = jnp.broadcast_to(jnp.max(m_ref[...], axis=-1, keepdims=True), m_ref.shape)

    @pl.loop(start, stop)
    def _(step):
        first_key = pl.multiple_of(step * block, block)
        values = v_ref[pl.ds(first_key, block), :]
        for head in range(groups):
            part = pl.ds(head * rows, rows)
            weights = jnp.exp2(s_ref[step, part, :] - m_ref[part, :1])
            total = l_ref[part, :]
            for piece in range(block // lanes):
                total = total + weights[:, piece * lanes:(piece + 1) * lanes]
            l_ref[part, :] = total
            acc_ref[part, :] += jnp.dot(
                weights.astype(jnp.bfloat16), values, preferred_element_type=jnp.float32
            )

    for head in range(groups):
        part = pl.ds(head * rows, rows)
        weight_sum = jnp.sum(l_ref[part, :], axis=-1, keepdims=True)
        out_ref[:, head * HS:(head + 1) * HS] = (acc_ref[part, :] / weight_sum).astype(out_ref.dtype)


def attend(queries, kv_rows, lo, bounds, kv_heads):
    rows, width = queries.shape
    all_rows = kv_rows.shape[0]
    groups = width // (kv_heads * HS)
    block = min(512, all_rows)
    wide = groups * HS
    return pl.pallas_call(
        functools.partial(attend_kernel, groups, block),
        out_shape=jax.ShapeDtypeStruct((rows, width), jnp.bfloat16),
        grid_spec=pltpu.PrefetchScalarGridSpec(
            num_scalar_prefetch=1,
            grid=(kv_heads,),
            in_specs=[
                pl.BlockSpec((rows, wide), lambda g, b: (0, g)),
                pl.BlockSpec((all_rows, HS), lambda g, b: (0, g)),
                pl.BlockSpec((all_rows, HS), lambda g, b: (0, kv_heads + g)),
                pl.BlockSpec((rows, 128), lambda g, b: (0, 0)),
            ],
            out_specs=pl.BlockSpec((rows, wide), lambda g, b: (0, g)),
            scratch_shapes=[
                pltpu.VMEM((all_rows // block, groups * rows, block), jnp.float32),
                pltpu.VMEM((groups * rows, 128), jnp.float32),
                pltpu.VMEM((groups * rows, 128), jnp.float32),
                pltpu.VMEM((groups * rows, HS), jnp.float32),
            ],
        ),
        compiler_params=pltpu.CompilerParams(
            dimension_semantics=("arbitrary",), vmem_limit_bytes=VMEM_LIMIT
        ),
        cost_estimate=pl.CostEstimate(
            flops=4 * rows * all_rows * width,
            bytes_accessed=2 * all_rows * kv_heads * HS * 2 + 4 * rows * width,
            transcendentals=rows * all_rows * width // HS,
        ),
        name="attend",
    )(bounds, queries, kv_rows, kv_rows, lo)


def gram_kernel(rin_ref, rout_ref, cin_ref, cout_ref, out_ref, rt_ref, mean_ref):
    all_rows, row_width = rin_ref.shape

    @pl.when(pl.program_id(0) == 0)
    def _():
        ones = jnp.ones((all_rows, 128), jnp.bfloat16)
        for source, ref in enumerate((rin_ref, rout_ref)):
            part = pl.ds(source * row_width, row_width)
            rt_ref[part, :] = ref[...].T
            mean_ref[part, :] = (
                jnp.dot(rt_ref[part, :], ones, preferred_element_type=jnp.float32) / all_rows
            )

    ones = jnp.ones((8, all_rows), jnp.bfloat16)
    for source, ref in enumerate((cin_ref, cout_ref)):
        cols = ref[...]
        col_mean = jnp.dot(ones, cols, preferred_element_type=jnp.float32)[:1] / all_rows
        gram = jnp.dot(rt_ref[...], cols, preferred_element_type=jnp.float32)
        cov = gram / all_rows - mean_ref[:, :1] * col_mean
        for row_source in range(2):
            out_ref[row_source, :, source, :] = cov[row_source * row_width:(row_source + 1) * row_width]


def joint_gram(rin, rout, cin, cout):
    all_rows, row_width = rin.shape
    col_width = cin.shape[1]
    tile = min(256, col_width)
    whole = pl.BlockSpec((all_rows, row_width), lambda j: (0, 0), pipeline_mode=pl.Buffered(1))
    strip = pl.BlockSpec((all_rows, tile), lambda j: (0, j))
    return pl.pallas_call(
        gram_kernel,
        out_shape=jax.ShapeDtypeStruct((2, row_width, 2, col_width), jnp.float32),
        grid=(col_width // tile,),
        in_specs=[whole, whole, strip, strip],
        out_specs=pl.BlockSpec((2, row_width, 2, tile), lambda j: (0, 0, 0, j)),
        scratch_shapes=[
            pltpu.VMEM((2 * row_width, all_rows), jnp.bfloat16),
            pltpu.VMEM((2 * row_width, 128), jnp.float32),
        ],
        compiler_params=pltpu.CompilerParams(
            dimension_semantics=("arbitrary",), vmem_limit_bytes=VMEM_LIMIT
        ),
        cost_estimate=pl.CostEstimate(
            flops=8 * all_rows * row_width * col_width,
            bytes_accessed=4 * all_rows * (row_width + col_width) + 16 * row_width * col_width,
            transcendentals=0,
        ),
        name="joint_gram",
    )(rin, rout, cin, cout)


def both_sides(block):
    if lax.axis_size("tp") != 2:
        return lax.all_gather(block, "tp", axis=1, tiled=True)
    other = lax.ppermute(block, "tp", ((0, 1), (1, 0)))
    first = lax.axis_index("tp") == 0
    return jnp.concatenate([jnp.where(first, block, other), jnp.where(first, other, block)], axis=1)


def on_device(hidden_in, norm_gain, w_query, w_key, w_value, w_out, doc_ids):
    tok_rows, col_width = hidden_in.shape
    tok_count = lax.axis_size("tok")
    tp_count = lax.axis_size("tp")
    tok_index = lax.axis_index("tok")
    all_rows = tok_rows * tok_count
    full_in = both_sides(hidden_in)
    widened = full_in.astype(jnp.float32)
    factor = lax.rsqrt(jnp.mean(widened * widened, axis=1, keepdims=True) + epsilon)
    normed = (widened * factor * norm_gain[None, :]).astype(jnp.bfloat16)
    kv_heads = w_key.shape[1] // HS
    groups = w_query.shape[1] // w_key.shape[1]
    first_row = tok_index * tok_rows
    positions = first_row + jnp.arange(tok_rows, dtype=jnp.int32)
    key_local = rotate(
        jnp.dot(normed, w_key, preferred_element_type=jnp.float32).reshape(tok_rows, kv_heads, HS),
        positions % all_rows,
    )
    key_local = key_local.astype(jnp.bfloat16).reshape(tok_rows, kv_heads * HS)
    value_local = jnp.dot(normed, w_value, preferred_element_type=jnp.float32).astype(jnp.bfloat16)
    kv_local = jnp.concatenate([key_local, value_local], axis=1)
    kv_rows = lax.all_gather(kv_local, "tok", axis=0, tiled=True)
    late_in, full_late, kv_rows = lax.optimization_barrier((hidden_in, full_in, kv_rows))
    cols_in = lax.all_gather(late_in, "tok", axis=0, tiled=True)
    rows_in = lax.all_to_all(full_in, "tok", 1, 0, tiled=True)
    queries = rotate(
        jnp.dot(normed, w_query, preferred_element_type=jnp.float32).reshape(
            tok_rows, kv_heads * groups, HS
        ),
        positions % all_rows,
    )
    queries = queries.astype(jnp.bfloat16).reshape(tok_rows, kv_heads * groups * HS)
    query_doc = lax.dynamic_slice_in_dim(doc_ids, first_row, tok_rows, 0)
    lo = jnp.sum((doc_ids[None, :] < query_doc[:, None]).astype(jnp.int32), axis=1)
    bounds = jnp.stack([first_row.astype(jnp.int32), lo[0]])
    attended = attend(queries, kv_rows, jnp.broadcast_to(lo[:, None], (tok_rows, 128)), bounds, kv_heads)
    partial_out = jnp.dot(attended, w_out, preferred_element_type=jnp.float32)
    if tp_count == 2:
        first = lax.axis_index("tp") == 0
        low, high = partial_out[:, :col_width], partial_out[:, col_width:]
        sent = jnp.where(first, high, low).astype(jnp.bfloat16)
        arrived = lax.ppermute(sent, "tp", ((0, 1), (1, 0)))
        summed = jnp.where(first, low, high) + arrived.astype(jnp.float32)
    else:
        summed = lax.psum_scatter(partial_out, "tp", scatter_dimension=1, tiled=True)
    hidden_out = (hidden_in.astype(jnp.float32) + summed).astype(jnp.bfloat16)
    cols_out = lax.all_gather(hidden_out, "tok", axis=0, tiled=True)
    rows_out = lax.all_to_all(both_sides(hidden_out), "tok", 1, 0, tiled=True)
    return (hidden_out, joint_gram(rows_in, rows_out, cols_in, cols_out))


def solution(mesh):
    return jax.shard_map(
        on_device,
        mesh=mesh,
        in_specs=(
            P("tok", "tp"),
            P(),
            P(None, "tp"),
            P(None, "tp"),
            P(None, "tp"),
            P("tp", None),
            P(),
        ),
        out_specs=(P("tok", "tp"), P(None, "tok", None, "tp")),
        check_vma=False,
    )
```

time: 591 us -> 484 us (0.82)
  blocking collectives: 0 us -> 91.6 us
  waiting for transfers between devices: 350 us -> 262 us
  matrix products: 103 us -> 20.3 us
  local copies, waits for them, and re-layouts: 68.9 us -> 5.15 us
  Pallas kernels: 0 us -> 40.3 us
  other arithmetic: 51.8 us -> 12.2 us
  starting transfers between devices: 0.42 us -> 38.2 us
    all_to_all x0 -> x1, blocking collectives: none -> 91.6 us  [on_device(): rows_out = lax.all_to_all(both_sides(hidden_out), 'tok', 1, 0, tiled=True)]
    all_gather x4 -> x3, waiting for transfers between devices: 241 us -> 152 us  [the longest x1 77.1 us: on_device(): cols_out = lax.all_gather(hidden_out, 'tok', axis=0, tiled=True)]
    dot_general x3 -> x0, matrix products: 78.5 us -> none  [the longest x1 28.9 us: on_device(): jnp.einsum('qhgd,khd->hgqk', queries, key_seq, preferred_element_type=jnp...]
    ppermute x0 -> x3, waiting for transfers between devices: none -> 70.8 us  [the longest x2 46.9 us: both_sides(): other = lax.ppermute(block, 'tp', ((0, 1), (1, 0)))]
    psum x1 -> x0, waiting for transfers between devices: 55.2 us -> none  [broadcast(): return lax.psum(block, axis)]
    reduce_scatter x1 -> x0, waiting for transfers between devices: 52.7 us -> none  [on_device(): lax.psum_scatter(partial_out, 'tp', scatter_dimension=1, tiled=True)]
    all_gather x1 -> x0, local copies, waits for them, and re-layouts: 40.5 us -> none  [on_device(): lax.all_gather(jnp.stack([hidden_in, hidden_out], axis=1), 'tok', axis=0,...]
    pallas_call x0 -> x2, Pallas kernels: none -> 40.3 us  [the longest x1 30.2 us: joint_gram(): pl.pallas_call(gram_kernel, out_shape=jax.ShapeDtypeStruct((2, row_width,...]
  transfers between devices with their start and end apart: 6 -> 7, of which waited for: 5 -> 6; matrix products, arithmetic and copies ran while one was open for 20% -> 6% of each run, Pallas kernels for 0% -> 2%
where the time goes in v1:
time: 484 us
  waiting for transfers between devices  262 us (54%)
  blocking collectives  91.6 us (19%)
  Pallas kernels  40.3 us (8%)
  starting transfers between devices  38.2 us (8%)
  matrix products  20.3 us (4%)
  between operations  14 us (3%)
  other arithmetic  12.2 us (3%)
  local copies, waits for them, and re-layouts  5.15 us (1%)
    all_to_all x1, blocking collectives, on_device(): rows_out = lax.all_to_all(both_sides(hidden_out), 'tok', 1, 0, tiled=True)  91.6 us
    all_gather x1, waiting for transfers between devices, on_device(): cols_out = lax.all_gather(hidden_out, 'tok', axis=0, tiled=True)  77.1 us
    all_gather x1, waiting for transfers between devices, on_device(): kv_rows = lax.all_gather(kv_local, 'tok', axis=0, tiled=True)  74.4 us
    ppermute x2, waiting for transfers between devices, both_sides(): other = lax.ppermute(block, 'tp', ((0, 1), (1, 0)))  46.9 us
    all_to_all x1, waiting for transfers between devices, on_device(): rows_in = lax.all_to_all(full_in, 'tok', 1, 0, tiled=True)  39.7 us
    all_to_all x1, starting transfers between devices, on_device(): rows_in = lax.all_to_all(full_in, 'tok', 1, 0, tiled=True)  31.9 us
    pallas_call x1, Pallas kernels, joint_gram(): pl.pallas_call(gram_kernel, out_shape=jax.ShapeDtypeStruct((2, row_width,...  30.2 us
    ppermute x1, waiting for transfers between devices, on_device(): arrived = lax.ppermute(sent, 'tp', ((0, 1), (1, 0)))  23.9 us
  transfers between devices with their start and end apart: 7, of which 6 were waited for; matrix products, arithmetic and copies ran while one was open for 6% of the time, Pallas kernels for 2%

profile of v1, /device:TPU:0, one launch (start us, length us, event | category | flops | bytes accessed | tf_op | source)
XLA Modules:
  0.0 483.8 jit_solution(2165904004325635547)
XLA Ops:
  7.2 0.0 all-gather.4.cloned.1.call-start
  7.2 3.0 collective-permute-start
  10.3 0.5 multiply_cosine_fusion
  10.8 22.9 %collective-permute-done = bf16[256,2048]{1,0:T(8,128)(2,1)} collective-permute-done((bf16[256,2048]{1,0:T(8,128)(2,1)}, bf16[256,2048]{1,0:T(8,128)(2,1)}, u32[]{:S(2)}, u32[]{:S(2)}) %collective-permute-start) | collective-permute-done | bytes 1048608 | tf_op jit(solution)/shard_map/ppermute | solution.py:180
  33.7 1.7 broadcast_select_fusion.3
  35.4 0.5 fusion
  35.9 0.0 copy-start.5
  35.9 2.0 convolution_convert_fusion
  37.9 0.2 copy-done.5
  38.1 1.3 fusion.6
  39.4 0.2 reshape.105
  39.6 0.5 subtract_convert_fusion.1
  40.1 0.4 pad_maximum_fusion.4
  40.5 1.8 pad_maximum_fusion.3
  42.3 0.0 all-gather.4.cloned.1.call-update
  42.4 0.0 all-gather.6.cloned.1.call-start
  42.4 1.5 pad_maximum_fusion
  43.9 74.4 %all-gather.4.cloned.1.call-done.k_ref.v_ref = bf16[4096,1024]{1,0:T(8,128)(2,1)} async-done(((bf16[256,1024]{1,0:T(8,128)(2,1)}), bf16[4096,1024]{1,0:T(8,128)(2,1)}) %all-gather.4.cloned.1.call-update) | async-done | bytes 8388624 | tf_op jit(solution)/shard_map/all_gather | solution.py:206
  118.3 0.0 all-gather.6.cloned.1.call-update
  118.3 0.2 all-gather.8.cloned.1.call-start
  118.6 0.1 dynamic_slice.3
  118.7 0.6 convert_reduce_fusion
  119.2 0.5 slice.21
  119.7 1.2 pad_add_fusion.bounds
  121.0 8.4 %convolution_bitcast_fusion = f32[32,8,16,128]{3,1,2,0:T(8,128)S(1)} fusion(bf16[4096,2048]{1,0:T(8,128)(2,1)} %param.9, f32[4096]{0:T(1024)S(1)} %copy-done.6, f32[256]{0:T(256)S(1)} %add_rsqrt_fusion, bf16[256,2048]{1,0:T(8,128)(2,1)S(1)} %get-tuple-element.11, bf16[256,2048]{1,0:T(8,128)(2,1)S(1)} %get-tuple-element.10), kind=kOutput, calls=%fused_computation.14 | convolution fusion | flops 4302307328 | bytes 20988928 | tf_op jit(solution)/shard_map/dot_general | solution.py:211
  129.4 0.4 copy.17
  129.8 0.8 subtract_convert_fusion
  130.6 0.6 pad_maximum_fusion.2
  131.1 1.2 copy.26
  132.4 0.7 broadcast_in_dim.2.lo_ref
  133.1 10.1 %attend.1 = bf16[256,2048]{1,0:T(8,128)(2,1)} custom-call(s32[2]{0:T(128)} %pad_add_fusion.bounds, bf16[256,2048]{1,0:T(8,128)(2,1)} %bitcast.39, bf16[4096,1024]{1,0:T(8,128)(2,1)} %all-gather.4.cloned.1.call-done.k_ref.v_ref, bf16[4096,1024]{1,0:T(8,128)(2,1)} %all-gather.4.cloned.1.call-done.k_ref.v_ref, s32[256,128]{1,0:T(8,128)} %broadcast_in_dim.2.lo_ref), custom_call_target="tpu_custom_call" | custom-call | flops 8589934592 | bytes 10485760 | tf_op jit(solution)/shard_map/attend/pallas_call | solution.py:94
  143.3 8.6 %fusion.9 = f32[256,4096]{1,0:T(8,128)S(1)} fusion(bf16[256,2048]{1,0:T(8,128)(2,1)} %attend.1, bf16[2048,4096]{1,0:T(8,128)(2,1)} %param.12), kind=kOutput, calls=%fused_computation.38 | convolution fusion | flops 4294967296 | bytes 22020096 | tf_op jit(solution)/shard_map/dot_general | solution.py:221
  151.9 0.2 select_convert_fusion
  152.1 1.4 collective-permute-start.1
  153.5 23.9 %collective-permute-done.1 = bf16[256,2048]{1,0:T(8,128)(2,1)S(1)} collective-permute-done((bf16[256,2048]{1,0:T(8,128)(2,1)S(1)}, bf16[256,2048]{1,0:T(8,128)(2,1)S(1)}, u32[]{:S(2)}, u32[]{:S(2)}) %collective-permute-start.1) | collective-permute-done | bytes 1048608 | tf_op jit(solution)/shard_map/ppermute | solution.py:226
  177.4 1.6 add_convert_fusion
  179.0 0.0 all-gather.8.cloned.1.call-update
  179.1 1.5 copy.25
  180.6 31.9 %all-to-all-start = ((bf16[256,16,256]{2,0,1:T(8,128)(2,1)}), bf16[256,16,256]{2,0,1:T(8,128)(2,1)}, u32[]{:S(2)}, u32[]{:S(2)}) async-start(bf16[256,16,256]{2,0,1:T(8,128)(2,1)} %bitcast.33), calls=%async_computation | async-start | bytes 4194304 | tf_op jit(solution)/shard_map/all_to_all | solution.py:209
  212.6 1.5 collective-permute-start.2
  214.1 24.0 %collective-permute-done.2 = bf16[256,2048]{1,0:T(8,128)(2,1)S(1)} collective-permute-done((bf16[256,2048]{1,0:T(8,128)(2,1)S(1)}, bf16[256,2048]{1,0:T(8,128)(2,1)S(1)}, u32[]{:S(2)}, u32[]{:S(2)}) %collective-permute-start.2) | collective-permute-done | bytes 1048608 | tf_op jit(solution)/shard_map/ppermute | solution.py:180
  238.0 0.1 broadcast_select_fusion.1
  238.2 0.2 pad_maximum_fusion.1
  238.4 0.2 copy.24
  238.6 39.7 %all-to-all-done = bf16[256,16,256]{2,0,1:T(8,128)(2,1)} async-done(((bf16[256,16,256]{2,0,1:T(8,128)(2,1)}), bf16[256,16,256]{2,0,1:T(8,128)(2,1)}, u32[]{:S(2)}, u32[]{:S(2)}) %all-to-all-start) | async-done | bytes 2097184 | tf_op jit(solution)/shard_map/all_to_all | solution.py:209
  278.3 91.6 %all_to_all.38 = bf16[256,16,256]{2,0,1:T(8,128)(2,1)} all-to-all(bf16[256,16,256]{2,0,1:T(8,128)(2,1)S(1)} %bitcast.34), channel_id=1, replica_groups=mesh['tok'=16,'tp'=2] {'tok'}, dimensions={1} | all-to-all | bytes 4194304 | tf_op jit(solution)/shard_map/all_to_all | solution.py:232
  370.0 77.1 %all-gather.8.cloned.1.call-done.cout_ref = bf16[4096,2048]{1,0:T(8,128)(2,1)} async-done(((bf16[256,2048]{1,0:T(8,128)(2,1)}), bf16[4096,2048]{1,0:T(8,128)(2,1)}) %all-gather.8.cloned.1.call-update) | async-done | bytes 16777232 | tf_op jit(solution)/shard_map/all_gather | solution.py:231
  447.0 30.2 %joint_gram.1 = f32[2,256,2,2048]{3,2,1,0:T(2,128)} custom-call(bf16[4096,256]{1,0:T(8,128)(2,1)} %bitcast.2.rin_ref, bf16[4096,256]{1,0:T(8,128)(2,1)} %bitcast.37, bf16[4096,2048]{1,0:T(8,128)(2,1)} %all-gather.6.cloned.1.call-done.cin_ref, bf16[4096,2048]{1,0:T(8,128)(2,1)} %all-gather.8.cloned.1.call-done.cout_ref), custom_call_target="tpu_custom_call" | custom-call | flops 17179869184 | bytes 46137344 | tf_op jit(solution)/shard_map/joint_gram/pallas_call | solution.py:155
  (17 shorter events, 0.1 us)
Async XLA Ops:
  7.2 28.8 %copy-start.6 = (f32[4096]{0:T(1024)S(1)}, f32[4096]{0:T(1024)}, u32[]{:S(2)}) copy-start(f32[4096]{0:T(1024)} %param.8) | copy-start | bytes 49156
  7.2 111.1 %all-gather.4.cloned.1.call-start = ((), (), s32[]{:S(2)}) async-start(), calls=%async_computation.2 | async-start | bytes 8912896 | tf_op jit(solution)/shard_map/all_gather | solution.py:206
  7.2 26.5 %collective-permute-start = (bf16[256,2048]{1,0:T(8,128)(2,1)}, bf16[256,2048]{1,0:T(8,128)(2,1)}, u32[]{:S(2)}, u32[]{:S(2)}) collective-permute-start(bf16[256,2048]{1,0:T(8,128)(2,1)} %param.7), channel_id=1, source_target_pairs={{0,1},{1,0},{2,3},{3,2},{4,5},{5,4},{6,7},{7,6},{8,9},{9,8},{10,11... | collective-permute-start | bytes 3145736 | tf_op jit(solution)/shard_map/ppermute | solution.py:180
  10.3 25.7 %copy-start.4 = (bf16[4096,512]{1,0:T(8,128)(2,1)S(1)}, bf16[4096,512]{1,0:T(8,128)(2,1)}, u32[]{:S(2)}) copy-start(bf16[4096,512]{1,0:T(8,128)(2,1)} %param.11) | copy-start | bytes 12582916
  35.9 2.2 copy-start.5
  40.1 78.4 %copy-start.3 = (s32[4096]{0:T(1024)S(1)}, s32[4096]{0:T(1024)}, u32[]{:S(2)}) copy-start(s32[4096]{0:T(1024)} %param.13) | copy-start | bytes 49156
  42.4 327.6 %all-gather.6.cloned.1.call-start = ((), (), s32[]{:S(2)}) async-start(), calls=%async_computation.3 | async-start | bytes 17825792 | tf_op jit(solution)/shard_map/all_gather | solution.py:208
  118.3 328.7 %all-gather.8.cloned.1.call-start = ((), (), s32[]{:S(2)}) async-start(), calls=%async_computation.4 | async-start | bytes 17825792 | tf_op jit(solution)/shard_map/all_gather | solution.py:231
  143.3 34.1 %copy-start = (bf16[256,2048]{1,0:T(8,128)(2,1)S(1)}, bf16[256,2048]{1,0:T(8,128)(2,1)}, u32[]{:S(2)}) copy-start(bf16[256,2048]{1,0:T(8,128)(2,1)} %param.7) | copy-start | bytes 3145732
  152.1 27.0 %copy-start.2 = (bf16[256,4096]{1,0:T(8,128)(2,1)S(1)}, bf16[256,4096]{1,0:T(8,128)(2,1)}, u32[]{:S(2)}) copy-start(bf16[256,4096]{1,0:T(8,128)(2,1)} %pad_maximum_fusion) | copy-start | bytes 6291460
  152.1 25.3 %collective-permute-start.1 = (bf16[256,2048]{1,0:T(8,128)(2,1)S(1)}, bf16[256,2048]{1,0:T(8,128)(2,1)S(1)}, u32[]{:S(2)}, u32[]{:S(2)}) collective-permute-start(bf16[256,2048]{1,0:T(8,128)(2,1)S(1)} %select_convert_fusion), channel_id=1, source_target_pairs={{0,1},{1,0},{2,3},{3,2},{4,5},{5,4},{6,7},{7,6},{8,9},{9,8},{10,11... | collective-permute-start | bytes 3145736 | tf_op jit(solution)/shard_map/ppermute | solution.py:226
  179.1 33.5 %copy-start.1 = (bf16[256,2048]{1,0:T(8,128)(2,1)S(1)}, bf16[256,2048]{1,0:T(8,128)(2,1)}, u32[]{:S(2)}) copy-start(bf16[256,2048]{1,0:T(8,128)(2,1)} %add_convert_fusion) | copy-start | bytes 3145732
  180.6 97.7 %all-to-all-start = ((bf16[256,16,256]{2,0,1:T(8,128)(2,1)}), bf16[256,16,256]{2,0,1:T(8,128)(2,1)}, u32[]{:S(2)}, u32[]{:S(2)}) async-start(bf16[256,16,256]{2,0,1:T(8,128)(2,1)} %bitcast.33), calls=%async_computation | async-start | bytes 4194304 | tf_op jit(solution)/shard_map/all_to_all | solution.py:209
  212.6 25.5 %collective-permute-start.2 = (bf16[256,2048]{1,0:T(8,128)(2,1)S(1)}, bf16[256,2048]{1,0:T(8,128)(2,1)S(1)}, u32[]{:S(2)}, u32[]{:S(2)}) collective-permute-start(bf16[256,2048]{1,0:T(8,128)(2,1)S(1)} %copy-done.1), channel_id=1, source_target_pairs={{0,1},{1,0},{2,3},{3,2},{4,5},{5,4},{6,7},{7,6},{8,9},{9,8},{10,11... | collective-permute-start | bytes 3145736 | tf_op jit(solution)/shard_map/ppermute | solution.py:180
Sparse Core Ops, SparseCore 0:
  42.5 75.7 all-gather.3
  120.5 158.2 all-gather.5
  281.5 165.4 all-gather.7

commit v2 on v1

--- a/solution.py
+++ b/solution.py
@@ -87,7 +87,7 @@
 
 def attend(queries, kv_rows, lo, bounds, kv_heads):
     rows, width = queries.shape
-    all_rows = kv_rows.shape[0]
+    all_rows = kv_rows.shape[1]
     groups = width // (kv_heads * HS)
     block = min(512, all_rows)
     wide = groups * HS
@@ -99,8 +99,8 @@
             grid=(kv_heads,),
             in_specs=[
                 pl.BlockSpec((rows, wide), lambda g, b: (0, g)),
-                pl.BlockSpec((all_rows, HS), lambda g, b: (0, g)),
-                pl.BlockSpec((all_rows, HS), lambda g, b: (0, kv_heads + g)),
+                pl.BlockSpec((None, all_rows, HS), lambda g, b: (0, 0, g)),
+                pl.BlockSpec((None, all_rows, HS), lambda g, b: (1, 0, g)),
                 pl.BlockSpec((rows, 128), lambda g, b: (0, 0)),
             ],
             out_specs=pl.BlockSpec((rows, wide), lambda g, b: (0, g)),
@@ -148,10 +148,12 @@
 
 def joint_gram(rin, rout, cin, cout):
     all_rows, row_width = rin.shape
-    col_width = cin.shape[1]
-    tile = min(256, col_width)
+    half = cin.shape[2]
+    col_width = 2 * half
+    tile = min(256, half)
+    strips = half // tile
     whole = pl.BlockSpec((all_rows, row_width), lambda j: (0, 0), pipeline_mode=pl.Buffered(1))
-    strip = pl.BlockSpec((all_rows, tile), lambda j: (0, j))
+    strip = pl.BlockSpec((None, all_rows, tile), lambda j: (j // strips, 0, j % strips))
     return pl.pallas_call(
         gram_kernel,
         out_shape=jax.ShapeDtypeStruct((2, row_width, 2, col_width), jnp.float32),
@@ -180,6 +182,141 @@
     other = lax.ppermute(block, "tp", ((0, 1), (1, 0)))
     first = lax.axis_index("tp") == 0
     return jnp.concatenate([jnp.where(first, block, other), jnp.where(first, other, block)], axis=1)
+
+
+def ring_kernel(chips, share, x_ref, *refs):
+    if share:
+        out_ref, side_ref, send, recv, psend, precv, local, ssend, srecv = refs
+    else:
+        out_ref, send, recv, psend, precv, local = refs
+    mesh_id = pl.DeviceIdType.MESH
+    rows = x_ref.shape[1]
+    me, tp = lax.axis_index("tok"), lax.axis_index("tp")
+    count = 2 * chips
+    core, chip = me % 2, me // 2
+    depth = chips // 2
+    spot = jnp.where(chip % 2 == 0, chip // 2, chips - 1 - chip // 2)
+
+    def device(place):
+        place = (place + 2 * chips) % chips
+        return jnp.where(place < depth, place * 4, (chips - 1 - place) * 4 + 2) + core
+
+    partner = me + 1 - 2 * core
+    ways = (device(spot + 1), device(spot - 1))
+    barrier = pltpu.get_barrier_semaphore()
+    for peer in (*ways, partner):
+        pl.semaphore_signal(barrier, inc=1, device_id={"tok": peer}, device_id_type=mesh_id)
+    if share:
+        for peer in range(count):
+            pl.semaphore_signal(barrier, inc=1, device_id={"tok": peer, "tp": 1 - tp}, device_id_type=mesh_id)
+    pl.semaphore_wait(barrier, 3 + (count if share else 0))
+
+    def block(way, origin):
+        return out_ref.at[way, pl.ds(pl.multiple_of(origin * rows, rows), rows), :]
+
+    pending = []
+
+    def step_copies(step, way):
+        origin = device(spot - step if way == 0 else spot + step)
+        source = x_ref.at[way] if step == 0 else block(way, origin)
+        ring = None
+        if step < chips - 1:
+            ring = pltpu.make_async_remote_copy(
+                src_ref=source, dst_ref=block(way, origin), send_sem=send.at[way, step],
+                recv_sem=recv.at[way, step], device_id={"tok": ways[way]}, device_id_type=mesh_id,
+            )
+            ring.start()
+        beside = pltpu.make_async_remote_copy(
+            src_ref=source, dst_ref=block(way, origin), send_sem=psend.at[way, step],
+            recv_sem=precv.at[way, step], device_id={"tok": partner}, device_id_type=mesh_id,
+        )
+        beside.start()
+        pending.append((ring, beside))
+        return ring
+
+    rings = [step_copies(0, way) for way in range(2)]
+    own = [pltpu.make_async_copy(x_ref.at[way], block(way, me), local.at[way]) for way in range(2)]
+    for copy in own:
+        copy.start()
+    sides = []
+    if share:
+        width = side_ref.shape[1]
+        per_half = x_ref.shape[2] // width
+        for j in range(count // 2):
+            copy = pltpu.make_async_remote_copy(
+                src_ref=x_ref.at[j // per_half, :, pl.ds(j % per_half * width, width)],
+                dst_ref=side_ref.at[pl.ds(pl.multiple_of(me * rows, rows), rows), :],
+                send_sem=ssend.at[j], recv_sem=srecv.at[me],
+                device_id={"tok": tp * (count // 2) + j, "tp": 1 - tp}, device_id_type=mesh_id,
+            )
+            copy.start()
+            sides.append(copy)
+    for step in range(1, chips):
+        for way in range(2):
+            rings[way].wait_recv()
+            rings[way] = step_copies(step, way)
+    for ring, beside in pending:
+        if ring is not None:
+            ring.wait_send()
+        beside.wait_send()
+        beside.wait_recv()
+    for copy in own:
+        copy.wait()
+    for copy in sides:
+        copy.wait_send()
+    if share:
+        @pl.when(me // (count // 2) != tp)
+        def _():
+            for sender in range(count):
+                landed = side_ref.at[pl.ds(sender * rows, rows), :]
+                pltpu.make_async_remote_copy(
+                    src_ref=landed, dst_ref=landed, send_sem=ssend.at[0], recv_sem=srecv.at[sender],
+                    device_id={"tok": sender, "tp": 1 - tp}, device_id_type=mesh_id,
+                ).wait_recv()
+
+
+def ring_gather(halves, share, call_id):
+    _, rows, width = halves.shape
+    count = lax.axis_size("tok")
+    chips = count // 2
+    out_shape = [jax.ShapeDtypeStruct((2, rows * count, width), halves.dtype)]
+    dma = pltpu.SemaphoreType.DMA
+    scratch = [dma((2, chips))] * 4 + [dma((2,))]
+    if share:
+        out_shape.append(jax.ShapeDtypeStruct((rows * count, 4 * width // count), halves.dtype))
+        scratch += [dma((count // 2,)), dma((count,))]
+    return pl.pallas_call(
+        functools.partial(ring_kernel, chips, share),
+        out_shape=out_shape,
+        in_specs=[pl.BlockSpec(memory_space=pltpu.VMEM)],
+        out_specs=[pl.BlockSpec(memory_space=pl.ANY)] * len(out_shape),
+        scratch_shapes=scratch,
+        compiler_params=pltpu.CompilerParams(
+            collective_id=call_id, has_side_effects=True, vmem_limit_bytes=8 * 1024 * 1024
+        ),
+        cost_estimate=pl.CostEstimate(
+            flops=40_000_000_000, bytes_accessed=2 * halves.size * count * 2, transcendentals=0
+        ),
+        name="ring_share" if share else "ring",
+    )(halves)
+
+
+def gather_halves(block):
+    rows, width = block.shape
+    halves = jnp.stack([block[:, : width // 2], block[:, width // 2 :]])
+    return lax.all_gather(halves, "tok", axis=1, tiled=True)
+
+
+def row_features(columns, arrived):
+    _, all_rows, half = columns.shape
+    row_width = 2 * half * lax.axis_size("tp") // lax.axis_size("tok")
+    first = lax.axis_index("tok") * row_width
+    offset, owner = first % (2 * half), first // (2 * half)
+    mine = lax.dynamic_slice(columns, (offset // half, 0, offset % half), (1, all_rows, row_width))[0]
+    owned = lax.axis_index("tp") == owner
+    if arrived is None:
+        return lax.psum(jnp.where(owned, mine, jnp.zeros_like(mine)), "tp")
+    return jnp.where(owned, mine, arrived)
 
 
 def on_device(hidden_in, norm_gain, w_query, w_key, w_value, w_out, doc_ids):
@@ -202,10 +339,8 @@
     )
     key_local = key_local.astype(jnp.bfloat16).reshape(tok_rows, kv_heads * HS)
     value_local = jnp.dot(normed, w_value, preferred_element_type=jnp.float32).astype(jnp.bfloat16)
-    kv_local = jnp.concatenate([key_local, value_local], axis=1)
-    kv_rows = lax.all_gather(kv_local, "tok", axis=0, tiled=True)
-    late_in, full_late, kv_rows = lax.optimization_barrier((hidden_in, full_in, kv_rows))
-    cols_in = lax.all_gather(late_in, "tok", axis=0, tiled=True)
+    (kv_rows,) = ring_gather(jnp.stack([key_local, value_local]), False, 0)
+    cols_in = gather_halves(hidden_in)
     rows_in = lax.all_to_all(full_in, "tok", 1, 0, tiled=True)
     queries = rotate(
         jnp.dot(normed, w_query, preferred_element_type=jnp.float32).reshape(
@@ -228,8 +363,13 @@
     else:
         summed = lax.psum_scatter(partial_out, "tp", scatter_dimension=1, tiled=True)
     hidden_out = (hidden_in.astype(jnp.float32) + summed).astype(jnp.bfloat16)
-    cols_out = lax.all_gather(hidden_out, "tok", axis=0, tiled=True)
-    rows_out = lax.all_to_all(both_sides(hidden_out), "tok", 1, 0, tiled=True)
+    halves = jnp.stack([hidden_out[:, : col_width // 2], hidden_out[:, col_width // 2 :]])
+    if tp_count == 2:
+        cols_out, arrived_rows = ring_gather(halves, True, 1)
+        rows_out = row_features(cols_out, arrived_rows)
+    else:
+        (cols_out,) = ring_gather(halves, False, 1)
+        rows_out = row_features(cols_out, None)
     return (hidden_out, joint_gram(rows_in, rows_out, cols_in, cols_out))
 
 

time: 484 us -> 454 us (0.938)
  Pallas kernels: 40.3 us -> 328 us
  waiting for transfers between devices: 262 us -> 20.2 us
  blocking collectives: 91.6 us -> 0 us
  local copies, waits for them, and re-layouts: 5.15 us -> 21.6 us
    pallas_call x0 -> x2, Pallas kernels: none -> 288 us  [ring_gather(): pl.pallas_call(functools.partial(ring_kernel, chips, share), out_shape=ou...]
    all_gather x3 -> x1, waiting for transfers between devices: 152 us -> 0.01 us  [gather_halves(): return lax.all_gather(halves, 'tok', axis=1, tiled=True)]
    all_to_all x1 -> x0, blocking collectives: 91.6 us -> none  [on_device(): rows_out = lax.all_to_all(both_sides(hidden_out), 'tok', 1, 0, tiled=True)]
    all_to_all x1, waiting for transfers between devices: 39.7 us -> 0.01 us  [on_device(): rows_in = lax.all_to_all(full_in, 'tok', 1, 0, tiled=True)]
    ppermute x2 -> x1, waiting for transfers between devices: 46.9 us -> 20.2 us  [both_sides(): other = lax.ppermute(block, 'tp', ((0, 1), (1, 0)))]
    ppermute x1, waiting for transfers between devices: 23.9 us -> 0.01 us  [on_device(): arrived = lax.ppermute(sent, 'tp', ((0, 1), (1, 0)))]
    unnamed x17 -> x22, local copies, waits for them, and re-layouts: 1.88 us -> 13.5 us
  transfers between devices with their start and end apart: 7 -> 4, of which waited for: 6 -> 1; matrix products, arithmetic and copies ran while one was open for 6% -> 10% of each run, Pallas kernels for 2% -> 65%
where the time goes in v2:
time: 454 us; the launch traced here: 455 us
  Pallas kernels  328 us (72%)
  starting transfers between devices  34.2 us (8%)
  local copies, waits for them, and re-layouts  21.6 us (5%)
  waiting for transfers between devices  20.2 us (4%)
  matrix products  20 us (4%)
  other arithmetic  16.8 us (4%)
  between operations  14.3 us (3%)
    pallas_call x2, Pallas kernels, ring_gather(): pl.pallas_call(functools.partial(ring_kernel, chips, share), out_shape=ou...  288 us
    pallas_call x1, Pallas kernels, joint_gram(): pl.pallas_call(gram_kernel, out_shape=jax.ShapeDtypeStruct((2, row_width,...  30.4 us
    all_to_all x1, starting transfers between devices, on_device(): rows_in = lax.all_to_all(full_in, 'tok', 1, 0, tiled=True)  29.5 us
    ppermute x1, waiting for transfers between devices, both_sides(): other = lax.ppermute(block, 'tp', ((0, 1), (1, 0)))  20.2 us
    unnamed x22, local copies, waits for them, and re-layouts  13.5 us
    pallas_call x1, Pallas kernels, attend(): pl.pallas_call(functools.partial(attend_kernel, groups, block), out_shape...  10.1 us
  transfers between devices with their start and end apart: 4, of which 1 were waited for; matrix products, arithmetic and copies ran while one was open for 10% of the time, Pallas kernels for 65%

profile of v2, /device:TPU:0, one launch (start us, length us, event | category | flops | bytes accessed | tf_op | source)
XLA Modules:
  0.0 455.1 jit_solution(6577316574156680488)
XLA Ops:
  7.2 0.0 all-gather.2.cloned.1.call-start
  7.2 1.3 slice_bitcast_fusion.3
  8.6 1.1 pad_maximum_fusion.3
  9.7 0.0 all-gather.2.cloned.1.call-update
  9.7 3.0 collective-permute-start
  12.7 0.1 dynamic_slice.6
  12.8 0.6 convert_reduce_fusion
  13.4 0.5 slice.33
  13.9 1.4 pad_add_fusion.bounds
  15.3 0.5 multiply_cosine_fusion
  15.8 20.2 %collective-permute-done = bf16[256,2048]{1,0:T(8,128)(2,1)} collective-permute-done((bf16[256,2048]{1,0:T(8,128)(2,1)S(1)}, bf16[256,2048]{1,0:T(8,128)(2,1)}, u32[]{:S(2)}, u32[]{:S(2)}) %collective-permute-start) | collective-permute-done | bytes 1048608 | tf_op jit(solution)/shard_map/ppermute | solution.py:182
  36.0 1.4 broadcast_select_fusion.1
  37.4 0.5 fusion
  37.9 2.1 fusion.7
  40.0 2.0 reshape.110
  42.0 1.7 subtract_convert_fusion.1
  43.7 1.1 pad_maximum_fusion.5
  44.8 1.8 convert_element_type.54
  46.5 8.2 %convolution_bitcast_fusion = f32[32,8,16,128]{3,1,2,0:T(8,128)S(1)} fusion(bf16[4096,2048]{1,0:T(8,128)(2,1)} %param.9, f32[4096]{0:T(1024)S(1)} %copy-done.9, f32[256]{0:T(256)S(1)} %add_rsqrt_fusion, bf16[256,2048]{1,0:T(8,128)(2,1)S(1)} %get-tuple-element.9, bf16[256,2048]{1,0:T(8,128)(2,1)S(1)} %get-tuple-element.8), kind=kOutput, calls=%fused_computation.13 | convolution fusion | flops 4302307328 | bytes 20988928 | tf_op jit(solution)/shard_map/dot_general | solution.py:346
  54.8 0.4 copy.12
  55.1 0.8 subtract_convert_fusion
  55.9 0.0 copy-start.8
  55.9 0.6 pad_maximum_fusion.1
  56.5 1.2 copy.17
  57.8 0.7 copy-done.8
  58.5 1.3 fusion.3
  59.8 0.1 pad_maximum_fusion.4.x_ref
  59.9 113.6 %ring.1.k_ref.v_ref = bf16[2,4096,512]{2,1,0:T(8,128)(2,1)S(1)} custom-call(bf16[2,256,512]{2,1,0:T(8,128)(2,1)S(1)} %pad_maximum_fusion.4.x_ref), custom_call_target="tpu_custom_call" | custom-call | flops 40000000000 | bytes 16777216 | tf_op jit(solution)/shard_map/ring/pallas_call | solution.py:288
  173.4 0.0 copy-start.1
  173.4 3.4 copy-done.1
  176.8 0.8 broadcast_in_dim.2.lo_ref
  177.6 10.1 %attend.1 = bf16[256,2048]{1,0:T(8,128)(2,1)} custom-call(s32[2]{0:T(128)} %pad_add_fusion.bounds, bf16[256,2048]{1,0:T(8,128)(2,1)} %bitcast.35, bf16[2,4096,512]{2,1,0:T(8,128)(2,1)} %copy-done.1, bf16[2,4096,512]{2,1,0:T(8,128)(2,1)} %copy-done.1, s32[256,128]{1,0:T(8,128)} %broadcast_in_dim.2.lo_ref), custom_call_target="tpu_custom_call" | custom-call | flops 8589934592 | bytes 10485760 | tf_op jit(solution)/shard_map/attend/pallas_call | solution.py:94
  187.7 8.4 %fusion.10 = f32[256,4096]{1,0:T(8,128)S(1)} fusion(bf16[256,2048]{1,0:T(8,128)(2,1)} %attend.1, bf16[2048,4096]{1,0:T(8,128)(2,1)} %param.12), kind=kOutput, calls=%fused_computation.41 | convolution fusion | flops 4294967296 | bytes 22020096 | tf_op jit(solution)/shard_map/dot_general | solution.py:356
  196.2 0.0 copy-start.2
  196.2 2.0 copy-done.2
  198.2 1.2 select_convert_fusion
  199.3 1.5 collective-permute-start.1
  200.9 0.1 pad_maximum_fusion
  201.0 1.5 copy.16
  202.5 29.5 %all-to-all-start = ((bf16[256,16,256]{2,0,1:T(8,128)(2,1)}), bf16[256,16,256]{2,0,1:T(8,128)(2,1)}, u32[]{:S(2)}, u32[]{:S(2)}) async-start(bf16[256,16,256]{2,0,1:T(8,128)(2,1)} %bitcast.30), calls=%async_computation | async-start | bytes 4194304 | tf_op jit(solution)/shard_map/all_to_all | solution.py:344
  232.1 3.2 add_convert_fusion
  235.2 0.0 copy-start.4
  235.3 0.1 slice_bitcast_fusion.1
  235.3 0.1 pad_maximum_fusion.2.x_ref
  235.4 174.1 %ring_share.1 = (bf16[2,4096,1024]{2,1,0:T(8,128)(2,1)S(1)}, bf16[4096,256]{1,0:T(8,128)(2,1)S(1)}) custom-call(bf16[2,256,1024]{2,1,0:T(8,128)(2,1)S(1)} %pad_maximum_fusion.2.x_ref), custom_call_target="tpu_custom_call" | custom-call | flops 40000000000 | bytes 33554432 | tf_op jit(solution)/shard_map/ring_share/pallas_call | solution.py:288
  409.6 5.7 %copy-done = bf16[2,4096,1024]{2,1,0:T(8,128)(2,1)} copy-done((bf16[2,4096,1024]{2,1,0:T(8,128)(2,1)}, bf16[2,4096,1024]{2,1,0:T(8,128)(2,1)S(1)}, u32[]{:S(2)}) %copy-start) | copy-done | bytes 16777240
  415.3 2.6 bitcast_select_fusion.rout_ref
  417.9 30.4 %joint_gram.1 = f32[2,256,2,2048]{3,2,1,0:T(2,128)} custom-call(bf16[4096,256]{1,0:T(8,128)(2,1)} %bitcast.3.rin_ref, bf16[4096,256]{1,0:T(8,128)(2,1)} %bitcast_select_fusion.rout_ref, bf16[2,4096,1024]{2,1,0:T(8,128)(2,1)} %all-gather.2.cloned.1.call-done.cin_ref, bf16[2,4096,1024]{2,1,0:T(8,128)(2,1)} %copy-done), custom_call_target="tpu_custom_call" | custom-call | flops 17179869184 | bytes 46137344 | tf_op jit(solution)/shard_map/joint_gram/pallas_call | solution.py:157
  (18 shorter events, 0.1 us)
Async XLA Ops:
  7.2 2.5 copy-start.3
  7.2 5.6 %copy-start.6 = (s32[4096]{0:T(1024)S(1)}, s32[4096]{0:T(1024)}, u32[]{:S(2)}) copy-start(s32[4096]{0:T(1024)} %param.13) | copy-start | bytes 49156
  7.2 410.7 %all-gather.2.cloned.1.call-start = ((), (), s32[]{:S(2)}) async-start(), calls=%async_computation.1 | async-start | bytes 17825792 | tf_op jit(solution)/shard_map/all_gather | solution.py:307
  9.7 28.2 %copy-start.9 = (f32[4096]{0:T(1024)S(1)}, f32[4096]{0:T(1024)}, u32[]{:S(2)}) copy-start(f32[4096]{0:T(1024)} %param.8) | copy-start | bytes 49156
  9.7 26.3 %collective-permute-start = (bf16[256,2048]{1,0:T(8,128)(2,1)S(1)}, bf16[256,2048]{1,0:T(8,128)(2,1)}, u32[]{:S(2)}, u32[]{:S(2)}) collective-permute-start(bf16[256,2048]{1,0:T(8,128)(2,1)S(1)} %copy-done.3), channel_id=1, source_target_pairs={{0,1},{1,0},{2,3},{3,2},{4,5},{5,4},{6,7},{7,6},{8,9},{9,8},{10,11... | collective-permute-start | bytes 3145736 | tf_op jit(solution)/shard_map/ppermute | solution.py:182
  12.7 25.2 %copy-start.7 = (bf16[4096,512]{1,0:T(8,128)(2,1)S(1)}, bf16[4096,512]{1,0:T(8,128)(2,1)}, u32[]{:S(2)}) copy-start(bf16[4096,512]{1,0:T(8,128)(2,1)} %param.10) | copy-start | bytes 12582916
  55.9 2.6 copy-start.8
  58.5 1.3 copy-start.5
  173.4 3.4 copy-start.1
  196.2 2.0 copy-start.2
  199.3 32.8 %collective-permute-start.1 = (bf16[256,2048]{1,0:T(8,128)(2,1)}, bf16[256,2048]{1,0:T(8,128)(2,1)}, u32[]{:S(2)}, u32[]{:S(2)}) collective-permute-start(bf16[256,2048]{1,0:T(8,128)(2,1)} %select_convert_fusion), channel_id=1, source_target_pairs={{0,1},{1,0},{2,3},{3,2},{4,5},{5,4},{6,7},{7,6},{8,9},{9,8},{10,11... | collective-permute-start | bytes 3145736 | tf_op jit(solution)/shard_map/ppermute | solution.py:361
  202.5 215.4 %all-to-all-start = ((bf16[256,16,256]{2,0,1:T(8,128)(2,1)}), bf16[256,16,256]{2,0,1:T(8,128)(2,1)}, u32[]{:S(2)}, u32[]{:S(2)}) async-start(bf16[256,16,256]{2,0,1:T(8,128)(2,1)} %bitcast.30), calls=%async_computation | async-start | bytes 4194304 | tf_op jit(solution)/shard_map/all_to_all | solution.py:344
  235.2 174.3 %copy-start.4 = (bf16[256,2048]{1,0:T(8,128)(2,1)}, bf16[256,2048]{1,0:T(8,128)(2,1)S(1)}, u32[]{:S(2)}) copy-start(bf16[256,2048]{1,0:T(8,128)(2,1)S(1)} %add_convert_fusion) | copy-start | bytes 3145732
  409.6 5.7 %copy-start = (bf16[2,4096,1024]{2,1,0:T(8,128)(2,1)}, bf16[2,4096,1024]{2,1,0:T(8,128)(2,1)S(1)}, u32[]{:S(2)}) copy-start(bf16[2,4096,1024]{2,1,0:T(8,128)(2,1)S(1)} %get-tuple-element.4.cout_ref) | copy-start | bytes 50331652
Sparse Core Ops, SparseCore 0:
  10.2 157.7 all-gather.1

commit v3 on v2

--- a/solution.py
+++ b/solution.py
@@ -123,7 +123,7 @@
     )(bounds, queries, kv_rows, kv_rows, lo)
 
 
-def gram_kernel(rin_ref, rout_ref, cin_ref, cout_ref, out_ref, rt_ref, mean_ref):
+def gram_kernel(strips, rin_ref, rout_ref, low_ref, high_ref, cout_ref, out_ref, rt_ref, mean_ref):
     all_rows, row_width = rin_ref.shape
 
     @pl.when(pl.program_id(0) == 0)
@@ -137,7 +137,8 @@
             )
 
     ones = jnp.ones((8, all_rows), jnp.bfloat16)
-    for source, ref in enumerate((cin_ref, cout_ref)):
+
+    def block(source, ref):
         cols = ref[...]
         col_mean = jnp.dot(ones, cols, preferred_element_type=jnp.float32)[:1] / all_rows
         gram = jnp.dot(rt_ref[...], cols, preferred_element_type=jnp.float32)
@@ -145,20 +146,32 @@
         for row_source in range(2):
             out_ref[row_source, :, source, :] = cov[row_source * row_width:(row_source + 1) * row_width]
 
+    @pl.when(pl.program_id(0) < strips)
+    def _():
+        block(0, low_ref)
+
+    @pl.when(pl.program_id(0) >= strips)
+    def _():
+        block(0, high_ref)
+
+    block(1, cout_ref)
+
 
 def joint_gram(rin, rout, cin, cout):
     all_rows, row_width = rin.shape
-    half = cin.shape[2]
+    half = cout.shape[2]
     col_width = 2 * half
     tile = min(256, half)
     strips = half // tile
     whole = pl.BlockSpec((all_rows, row_width), lambda j: (0, 0), pipeline_mode=pl.Buffered(1))
     strip = pl.BlockSpec((None, all_rows, tile), lambda j: (j // strips, 0, j % strips))
+    low = pl.BlockSpec((all_rows, tile), lambda j: (0, jnp.minimum(j, strips - 1)))
+    high = pl.BlockSpec((all_rows, tile), lambda j: (0, jnp.maximum(j - strips, 0)))
     return pl.pallas_call(
-        gram_kernel,
+        functools.partial(gram_kernel, strips),
         out_shape=jax.ShapeDtypeStruct((2, row_width, 2, col_width), jnp.float32),
         grid=(col_width // tile,),
-        in_specs=[whole, whole, strip, strip],
+        in_specs=[whole, whole, low, high, strip],
         out_specs=pl.BlockSpec((2, row_width, 2, tile), lambda j: (0, 0, 0, j)),
         scratch_shapes=[
             pltpu.VMEM((2 * row_width, all_rows), jnp.bfloat16),
@@ -173,7 +186,7 @@
             transcendentals=0,
         ),
         name="joint_gram",
-    )(rin, rout, cin, cout)
+    )(rin, rout, *cin, cout)
 
 
 def both_sides(block):
@@ -207,9 +220,8 @@
     for peer in (*ways, partner):
         pl.semaphore_signal(barrier, inc=1, device_id={"tok": peer}, device_id_type=mesh_id)
     if share:
-        for peer in range(count):
-            pl.semaphore_signal(barrier, inc=1, device_id={"tok": peer, "tp": 1 - tp}, device_id_type=mesh_id)
-    pl.semaphore_wait(barrier, 3 + (count if share else 0))
+        pl.semaphore_signal(barrier, inc=1, device_id={"tp": 1 - tp}, device_id_type=mesh_id)
+    pl.semaphore_wait(barrier, 4 if share else 3)
 
     def block(way, origin):
         return out_ref.at[way, pl.ds(pl.multiple_of(origin * rows, rows), rows), :]
@@ -238,41 +250,58 @@
     own = [pltpu.make_async_copy(x_ref.at[way], block(way, me), local.at[way]) for way in range(2)]
     for copy in own:
         copy.start()
-    sides = []
     if share:
         width = side_ref.shape[1]
-        per_half = x_ref.shape[2] // width
-        for j in range(count // 2):
-            copy = pltpu.make_async_remote_copy(
-                src_ref=x_ref.at[j // per_half, :, pl.ds(j % per_half * width, width)],
-                dst_ref=side_ref.at[pl.ds(pl.multiple_of(me * rows, rows), rows), :],
-                send_sem=ssend.at[j], recv_sem=srecv.at[me],
-                device_id={"tok": tp * (count // 2) + j, "tp": 1 - tp}, device_id_type=mesh_id,
-            )
-            copy.start()
-            sides.append(copy)
+        half = x_ref.shape[2]
+        owner = me // (count // 2)
+        my_way = me * width % (2 * half) // half
+        features = pl.ds(pl.multiple_of(me * width % half, width), width)
+
+    def side_copy(step, way, kind):
+        origin = device(spot - step if way == 0 else spot + step)
+        origin = origin + kind * (1 - 2 * core)
+        source = x_ref.at[way, :, features]
+        if step > 0 or kind > 0:
+            source = out_ref.at[way, pl.ds(pl.multiple_of(origin * rows, rows), rows), features]
+        return pltpu.make_async_remote_copy(
+            src_ref=source,
+            dst_ref=side_ref.at[pl.ds(pl.multiple_of(origin * rows, rows), rows), :],
+            send_sem=ssend.at[kind, step], recv_sem=srecv.at[kind, step],
+            device_id={"tp": 1 - tp}, device_id_type=mesh_id,
+        )
+
+    def each_side(act, step, way, kind, holder):
+        if share:
+            @pl.when((my_way == way) & ((owner == tp) == holder))
+            def _():
+                act(side_copy(step, way, kind))
+
+    def start(copy):
+        copy.start()
+
+    for way in range(2):
+        each_side(start, 0, way, 0, True)
     for step in range(1, chips):
         for way in range(2):
             rings[way].wait_recv()
             rings[way] = step_copies(step, way)
+            each_side(start, step, way, 0, True)
+            pending[2 * (step - 1) + way][1].wait_recv()
+            each_side(start, step - 1, way, 1, True)
+    for way in range(2):
+        pending[2 * (chips - 1) + way][1].wait_recv()
+        each_side(start, chips - 1, way, 1, True)
     for ring, beside in pending:
         if ring is not None:
             ring.wait_send()
         beside.wait_send()
-        beside.wait_recv()
     for copy in own:
         copy.wait()
-    for copy in sides:
-        copy.wait_send()
-    if share:
-        @pl.when(me // (count // 2) != tp)
-        def _():
-            for sender in range(count):
-                landed = side_ref.at[pl.ds(sender * rows, rows), :]
-                pltpu.make_async_remote_copy(
-                    src_ref=landed, dst_ref=landed, send_sem=ssend.at[0], recv_sem=srecv.at[sender],
-                    device_id={"tok": sender, "tp": 1 - tp}, device_id_type=mesh_id,
-                ).wait_recv()
+    for step in range(chips):
+        for way in range(2):
+            for kind in range(2):
+                each_side(lambda copy: copy.wait_send(), step, way, kind, True)
+                each_side(lambda copy: copy.wait_recv(), step, way, kind, False)
 
 
 def ring_gather(halves, share, call_id):
@@ -284,7 +313,7 @@
     scratch = [dma((2, chips))] * 4 + [dma((2,))]
     if share:
         out_shape.append(jax.ShapeDtypeStruct((rows * count, 4 * width // count), halves.dtype))
-        scratch += [dma((count // 2,)), dma((count,))]
+        scratch += [dma((2, chips))] * 2
     return pl.pallas_call(
         functools.partial(ring_kernel, chips, share),
         out_shape=out_shape,
@@ -292,19 +321,13 @@
         out_specs=[pl.BlockSpec(memory_space=pl.ANY)] * len(out_shape),
         scratch_shapes=scratch,
         compiler_params=pltpu.CompilerParams(
-            collective_id=call_id, has_side_effects=True, vmem_limit_bytes=8 * 1024 * 1024
+            collective_id=call_id, has_side_effects=True, vmem_limit_bytes=VMEM_LIMIT
         ),
         cost_estimate=pl.CostEstimate(
             flops=40_000_000_000, bytes_accessed=2 * halves.size * count * 2, transcendentals=0
         ),
         name="ring_share" if share else "ring",
     )(halves)
-
-
-def gather_halves(block):
-    rows, width = block.shape
-    halves = jnp.stack([block[:, : width // 2], block[:, width // 2 :]])
-    return lax.all_gather(halves, "tok", axis=1, tiled=True)
 
 
 def row_features(columns, arrived):
@@ -340,7 +363,9 @@
     key_local = key_local.astype(jnp.bfloat16).reshape(tok_rows, kv_heads * HS)
     value_local = jnp.dot(normed, w_value, preferred_element_type=jnp.float32).astype(jnp.bfloat16)
     (kv_rows,) = ring_gather(jnp.stack([key_local, value_local]), False, 0)
-    cols_in = gather_halves(hidden_in)
+    early, late = hidden_in[:, : col_width // 2], hidden_in[:, col_width // 2 :]
+    late, kv_rows = lax.optimization_barrier((late, kv_rows))
+    cols_in = [lax.all_gather(part, "tok", axis=0, tiled=True) for part in (early, late)]
     rows_in = lax.all_to_all(full_in, "tok", 1, 0, tiled=True)
     queries = rotate(
         jnp.dot(normed, w_query, preferred_element_type=jnp.float32).reshape(

time: 454 us -> 382 us (0.84)
  Pallas kernels: 328 us -> 268 us
  local copies, waits for them, and re-layouts: 21.6 us -> 9.14 us
  starting transfers between devices: 34.2 us -> 28.1 us
    pallas_call x2, Pallas kernels: 288 us -> 225 us  [ring_gather(): pl.pallas_call(functools.partial(ring_kernel, chips, share), out_shape=ou...]
    unnamed x22 -> x14, local copies, waits for them, and re-layouts: 13.5 us -> 3.66 us
    all_to_all x1, starting transfers between devices: 29.5 us -> 22.9 us  [on_device(): rows_in = lax.all_to_all(full_in, 'tok', 1, 0, tiled=True)]
  transfers between devices with their start and end apart: 4 -> 5, of which waited for: 1 -> 1; matrix products, arithmetic and copies ran while one was open for 10% -> 11% of each run, Pallas kernels for 65% -> 62%
where the time goes in v3:
time: 382 us; the launch traced here: 381 us
  Pallas kernels  268 us (70%)
  starting transfers between devices  28.1 us (7%)
  waiting for transfers between devices  23 us (6%)
  matrix products  21.8 us (6%)
  other arithmetic  16.9 us (4%)
  between operations  14.3 us (4%)
  local copies, waits for them, and re-layouts  9.14 us (2%)
    pallas_call x2, Pallas kernels, ring_gather(): pl.pallas_call(functools.partial(ring_kernel, chips, share), out_shape=ou...  225 us
    pallas_call x1, Pallas kernels, joint_gram(): pl.pallas_call(functools.partial(gram_kernel, strips), out_shape=jax.Shap...  32.3 us
    ppermute x1, waiting for transfers between devices, both_sides(): other = lax.ppermute(block, 'tp', ((0, 1), (1, 0)))  22.9 us
    all_to_all x1, starting transfers between devices, on_device(): rows_in = lax.all_to_all(full_in, 'tok', 1, 0, tiled=True)  22.9 us
    pallas_call x1, Pallas kernels, attend(): pl.pallas_call(functools.partial(attend_kernel, groups, block), out_shape...  10.1 us
    dot_general x1, matrix products, on_device(): jnp.dot(normed, w_query, preferred_element_type=jnp.float32)  8.57 us
    dot_general x1, matrix products, on_device(): partial_out = jnp.dot(attended, w_out, preferred_element_type=jnp.float32)  8.42 us
  transfers between devices with their start and end apart: 5, of which 1 were waited for; matrix products, arithmetic and copies ran while one was open for 11% of the time, Pallas kernels for 62%

profile of v3, /device:TPU:0, one launch (start us, length us, event | category | flops | bytes accessed | tf_op | source)
XLA Modules:
  0.0 380.8 jit_solution(14503733692742604877)
XLA Ops:
  7.2 0.0 all-gather.3.cloned.1.call-start
  7.2 2.2 fusion.10
  9.5 0.0 all-gather.3.cloned.1.call-update
  9.5 0.0 all-gather.5.cloned.1.call-start
  9.5 3.0 collective-permute-start
  12.6 0.5 multiply_cosine_fusion
  13.1 22.9 %collective-permute-done = bf16[256,2048]{1,0:T(8,128)(2,1)} collective-permute-done((bf16[256,2048]{1,0:T(8,128)(2,1)}, bf16[256,2048]{1,0:T(8,128)(2,1)}, u32[]{:S(2)}, u32[]{:S(2)}) %collective-permute-start) | collective-permute-done | bytes 1048608 | tf_op jit(solution)/shard_map/ppermute | solution.py:195
  36.0 1.7 broadcast_select_fusion.1
  37.7 0.5 fusion
  38.2 0.0 copy-done.5
  38.2 1.3 fusion.7
  39.5 0.2 reshape.110
  39.7 0.5 subtract_convert_fusion.1
  40.2 0.4 pad_maximum_fusion.4
  40.6 0.1 convert_element_type.54
  40.7 3.5 fusion.3
  44.2 0.8 pad_maximum_fusion.3.x_ref
  45.1 85.2 %ring.1.k_ref.v_ref = bf16[2,4096,512]{2,1,0:T(8,128)(2,1)} custom-call(bf16[2,256,512]{2,1,0:T(8,128)(2,1)} %pad_maximum_fusion.3.x_ref), custom_call_target="tpu_custom_call" | custom-call | flops 40000000000 | bytes 16777216 | tf_op jit(solution)/shard_map/ring/pallas_call | solution.py:317
  130.3 0.0 all-gather.5.cloned.1.call-update
  130.3 0.1 dynamic_slice.6
  130.4 0.6 convert_reduce_fusion
  130.9 0.5 slice.33
  131.5 1.3 pad_add_fusion.bounds
  132.7 8.6 %convolution_bitcast_fusion = f32[32,8,16,128]{3,1,2,0:T(8,128)S(1)} fusion(bf16[4096,2048]{1,0:T(8,128)(2,1)} %param.9, f32[4096]{0:T(1024)S(1)} %copy-done.5, f32[256]{0:T(256)S(1)} %add_rsqrt_fusion, bf16[256,2048]{1,0:T(8,128)(2,1)S(1)} %get-tuple-element.13, bf16[256,2048]{1,0:T(8,128)(2,1)S(1)} %get-tuple-element.12), kind=kOutput, calls=%fused_computation.13 | convolution fusion | flops 4302307328 | bytes 20988928 | tf_op jit(solution)/shard_map/dot_general | solution.py:371
  141.3 0.4 copy.12
  141.7 0.8 subtract_convert_fusion
  142.5 0.6 pad_maximum_fusion.1
  143.1 1.2 copy.17
  144.3 0.8 broadcast_in_dim.2.lo_ref
  145.1 10.1 %attend.1 = bf16[256,2048]{1,0:T(8,128)(2,1)} custom-call(s32[2]{0:T(128)} %pad_add_fusion.bounds, bf16[256,2048]{1,0:T(8,128)(2,1)} %bitcast.31, bf16[2,4096,512]{2,1,0:T(8,128)(2,1)} %ring.1.k_ref.v_ref, bf16[2,4096,512]{2,1,0:T(8,128)(2,1)} %ring.1.k_ref.v_ref, s32[256,128]{1,0:T(8,128)} %broadcast_in_dim.2.lo_ref), custom_call_target="tpu_custom_call" | custom-call | flops 8589934592 | bytes 10485760 | tf_op jit(solution)/shard_map/attend/pallas_call | solution.py:94
  155.2 8.4 %fusion.11 = f32[256,4096]{1,0:T(8,128)S(1)} fusion(bf16[256,2048]{1,0:T(8,128)(2,1)} %attend.1, bf16[2048,4096]{1,0:T(8,128)(2,1)} %param.12), kind=kOutput, calls=%fused_computation.39 | convolution fusion | flops 4294967296 | bytes 22020096 | tf_op jit(solution)/shard_map/dot_general | solution.py:381
  163.6 0.0 copy-start
  163.6 2.0 copy-done
  165.6 0.2 select_convert_fusion
  165.8 2.1 collective-permute-start.1
  167.9 0.2 pad_maximum_fusion
  168.1 0.0 copy-start.1
  168.1 1.5 copy.16
  169.6 22.9 %all-to-all-start = ((bf16[256,16,256]{2,0,1:T(8,128)(2,1)}), bf16[256,16,256]{2,0,1:T(8,128)(2,1)}, u32[]{:S(2)}, u32[]{:S(2)}) async-start(bf16[256,16,256]{2,0,1:T(8,128)(2,1)} %bitcast.26), calls=%async_computation | async-start | bytes 4194304 | tf_op jit(solution)/shard_map/all_to_all | solution.py:369
  192.5 0.0 collective-permute-done.1
  192.5 3.2 add_convert_fusion
  195.7 0.0 copy-start.2
  195.7 0.1 slice_bitcast_fusion.1
  195.8 1.2 pad_maximum_fusion.2.x_ref
  197.0 140.1 %ring_share.1 = (bf16[2,4096,1024]{2,1,0:T(8,128)(2,1)}, bf16[4096,256]{1,0:T(8,128)(2,1)}) custom-call(bf16[2,256,1024]{2,1,0:T(8,128)(2,1)} %pad_maximum_fusion.2.x_ref), custom_call_target="tpu_custom_call" | custom-call | flops 40000000000 | bytes 33554432 | tf_op jit(solution)/shard_map/ring_share/pallas_call | solution.py:317
  337.1 4.5 %bitcast_select_fusion.rout_ref = bf16[4096,256]{1,0:T(8,128)(2,1)} fusion(bf16[4096,256]{1,0:T(8,128)(2,1)} %get-tuple-element.8, bf16[2,4096,1024]{2,1,0:T(8,128)(2,1)} %get-tuple-element.7.cout_ref, s32[]{:T(128)S(6)} %select_n.80, s32[]{:T(128)S(6)} %select_n.82, pred[]{:T(512)S(6)} %eq.14), kind=kLoop, calls=%fused_computation.8 | loop fusion | flops 1048576 | bytes 6291465 | tf_op jit(solution)/shard_map/jit(_where)/select_n | solution.py:342
  341.6 0.0 all-to-all-done
  341.7 32.3 %joint_gram.1 = f32[2,256,2,2048]{3,2,1,0:T(2,128)} custom-call(bf16[4096,256]{1,0:T(8,128)(2,1)} %bitcast.3.rin_ref, bf16[4096,256]{1,0:T(8,128)(2,1)} %bitcast_select_fusion.rout_ref, bf16[4096,1024]{1,0:T(8,128)(2,1)} %all-gather.3.cloned.1.call-done.low_ref, bf16[4096,1024]{1,0:T(8,128)(2,1)} %all-gather.5.cloned.1.call-done.high_ref, ...), custom_call_target="tpu_custom_call" | custom-call | flops 17179869184 | bytes 46137344 | tf_op jit(solution)/shard_map/joint_gram/pallas_call | solution.py:170
  (12 shorter events, 0.0 us)
Async XLA Ops:
  7.2 31.1 %copy-start.5 = (f32[4096]{0:T(1024)S(1)}, f32[4096]{0:T(1024)}, u32[]{:S(2)}) copy-start(f32[4096]{0:T(1024)} %param.8) | copy-start | bytes 49156
  7.2 334.5 %all-gather.3.cloned.1.call-start = ((), (), s32[]{:S(2)}) async-start(), calls=%async_computation.1 | async-start | bytes 8912896 | tf_op jit(solution)/shard_map/all_gather | solution.py:368
  9.5 332.2 %all-gather.5.cloned.1.call-start = ((), (), s32[]{:S(2)}) async-start(), calls=%async_computation.2 | async-start | bytes 8912896 | tf_op jit(solution)/shard_map/all_gather | solution.py:368
  9.5 26.5 %collective-permute-start = (bf16[256,2048]{1,0:T(8,128)(2,1)}, bf16[256,2048]{1,0:T(8,128)(2,1)}, u32[]{:S(2)}, u32[]{:S(2)}) collective-permute-start(bf16[256,2048]{1,0:T(8,128)(2,1)} %param.7), channel_id=1, source_target_pairs={{0,1},{1,0},{2,3},{3,2},{4,5},{5,4},{6,7},{7,6},{8,9},{9,8},{10,11... | collective-permute-start | bytes 3145736 | tf_op jit(solution)/shard_map/ppermute | solution.py:195
  12.6 25.7 %copy-start.4 = (bf16[4096,512]{1,0:T(8,128)(2,1)S(1)}, bf16[4096,512]{1,0:T(8,128)(2,1)}, u32[]{:S(2)}) copy-start(bf16[4096,512]{1,0:T(8,128)(2,1)} %param.10) | copy-start | bytes 12582916
  45.0 85.2 %copy-start.3 = (s32[4096]{0:T(1024)S(1)}, s32[4096]{0:T(1024)}, u32[]{:S(2)}) copy-start(s32[4096]{0:T(1024)} %param.13) | copy-start | bytes 49156
  163.6 2.0 copy-start
  165.8 26.7 %collective-permute-start.1 = (bf16[256,2048]{1,0:T(8,128)(2,1)S(1)}, bf16[256,2048]{1,0:T(8,128)(2,1)}, u32[]{:S(2)}, u32[]{:S(2)}) collective-permute-start(bf16[256,2048]{1,0:T(8,128)(2,1)S(1)} %select_convert_fusion), channel_id=1, source_target_pairs={{0,1},{1,0},{2,3},{3,2},{4,5},{5,4},{6,7},{7,6},{8,9},{9,8},{10,11... | collective-permute-start | bytes 3145736 | tf_op jit(solution)/shard_map/ppermute | solution.py:386
  168.1 24.4 %copy-start.1 = (bf16[256,2048]{1,0:T(8,128)(2,1)S(1)}, bf16[256,2048]{1,0:T(8,128)(2,1)}, u32[]{:S(2)}) copy-start(bf16[256,2048]{1,0:T(8,128)(2,1)} %param.7) | copy-start | bytes 3145732
  169.6 172.0 %all-to-all-start = ((bf16[256,16,256]{2,0,1:T(8,128)(2,1)}), bf16[256,16,256]{2,0,1:T(8,128)(2,1)}, u32[]{:S(2)}, u32[]{:S(2)}) async-start(bf16[256,16,256]{2,0,1:T(8,128)(2,1)} %bitcast.26), calls=%async_computation | async-start | bytes 4194304 | tf_op jit(solution)/shard_map/all_to_all | solution.py:369
  195.7 141.4 %copy-start.2 = (bf16[256,2048]{1,0:T(8,128)(2,1)}, bf16[256,2048]{1,0:T(8,128)(2,1)S(1)}, u32[]{:S(2)}) copy-start(bf16[256,2048]{1,0:T(8,128)(2,1)S(1)} %add_convert_fusion) | copy-start | bytes 3145732
Sparse Core Ops, SparseCore 0:
  10.1 92.3 all-gather.2
  130.4 88.5 all-gather.4
